TPU v7x, 32 devices: a whole 2x2x4 slice. The times are simulated.
32 devices in a mesh: gx: 8 (over y, x, core), gy: 4 (over z).
Axes of the slice: x: 2, y: 2, z: 4, core: 2. Of those that a mesh axis runs over, the one named last changes fastest.
Arguments:
- permeability: float32 [8192, 1024], P('gx', 'gy'), may hold values from 0.01 to 100
- basis: float32 [64, 8, 256, 256], P('gx', 'gy'), may hold values from 0 to 1, as said below
- support: int32 [64, 8, 256, 256], P('gx', 'gy'), may hold values from 0 to 1, as said below
Outputs:
- smoothed: float32 [64, 8, 256, 256], P('gx', 'gy')
Inputs may be any that keep to these rules, and one draw needn't show every extreme that they name: support is 1 exactly on a rectangle of the box that contains the block's own 128 x 128 cells in its middle and reaches 32 to 64 cells past them on each side, cut to the grid. basis is positive where support is 1 and 0 elsewhere.
All inputs are finite; a program needn't handle non-finite values.
Results may differ from a plain program's by a relative error of at most 0.0003.
Values sent between devices are 32-bit elements; how exact they have to be, the bound alone decides.
A program may use at most 128 MiB of HBM per device.

v0:
```python
import jax
import jax.numpy as jnp
from jax import lax
from jax.sharding import PartitionSpec as P

B = 128
ITERS = 2


relaxation = 2.0 / 3.0


def shifted(block, axis, distance):
    devices = range(lax.axis_size(axis))
    route = [(i - distance, i) for i in devices if i - distance in devices]
    return lax.ppermute(block, axis, route)


def padded_2(shard, sides, width):
    for axis, dim in sides:
        devices, length = (lax.axis_size(axis), shard.shape[dim])
        up = [(i, (i + 1) % devices) for i in range(devices - 1)]
        down = [(j, i) for i, j in up]
        last = lax.slice_in_dim(shard, length - width, length, axis=dim)
        initial = lax.slice_in_dim(shard, 0, width, axis=dim)
        before = lax.ppermute(last, axis, up)
        after = lax.ppermute(initial, axis, down)
        shard = jnp.concatenate([before, shard, after], axis=dim)
    return shard


def to_wide(extended, count_x, count_y, block):
    tiles = extended.reshape(count_x + 1, block, count_y + 1, block)
    rows = jnp.concatenate([tiles[:-1], tiles[1:]], axis=1)
    return jnp.concatenate([rows[:, :, :-1], rows[:, :, 1:]], axis=3)


def from_wide(boxes, block):
    count_x, count_y = (boxes.shape[0], boxes.shape[2])
    none = (0, 0)
    tiles = jnp.pad(boxes[:, :block, :, :block], ((0, 1), none, (0, 1), none))
    tiles = tiles + jnp.pad(boxes[:, :block, :, block:], ((0, 1), none, (1, 0), none))
    tiles = tiles + jnp.pad(boxes[:, block:, :, :block], ((1, 0), none, (0, 1), none))
    tiles = tiles + jnp.pad(boxes[:, block:, :, block:], ((1, 0), none, (1, 0), none))
    return tiles.reshape((count_x + 1) * block, (count_y + 1) * block)


def harmonic(left, right):
    summed = left + right
    inside = summed > 0
    return jnp.where(inside, 2.0 * left * right / jnp.where(inside, summed, 1.0), 0.0)


def couplings(padded):
    faces_x = harmonic(padded[:-1, 1:-1], padded[1:, 1:-1])
    faces_y = harmonic(padded[1:-1, :-1], padded[1:-1, 1:])
    east = faces_x[1:]
    west = faces_x[:-1]
    north = faces_y[:, 1:]
    south = faces_y[:, :-1]
    diagonal = east + west + north + south
    return (east, west, north, south, jnp.where(diagonal > 0, diagonal, 1.0))


def smooth(basis, inside, east, west, north, south, diagonal):
    none = (0, 0)
    from_east = jnp.pad(basis[:, 1:], (none, (0, 1), none, none))
    from_west = jnp.pad(basis[:, :-1], (none, (1, 0), none, none))
    from_north = jnp.pad(basis[:, :, :, 1:], (none, none, none, (0, 1)))
    from_south = jnp.pad(basis[:, :, :, :-1], (none, none, none, (1, 0)))
    coupled = east * from_east + west * from_west + north * from_north + south * from_south
    return jnp.where(inside, (1.0 - relaxation) * basis + relaxation * coupled / diagonal, 0.0)


def add_ends(field, lower_in, upper_in, width, axis):
    length = field.shape[axis]
    if axis == 0:
        head = field[:width] + lower_in
        middle = field[width : length - width]
        tail = field[length - width :] + upper_in
    else:
        head = field[:, :width] + lower_in
        middle = field[:, width : length - width]
        tail = field[:, length - width :] + upper_in
    return jnp.concatenate([head, middle, tail], axis=axis)


def send_first(strip, offset):
    return shifted(strip, "gx", offset)


def send_second(strip, offset):
    return shifted(strip, "gy", offset)


def local(permeability, basis, support):
    block = B
    margin = block // 2
    count_x, count_y = (basis.shape[0], basis.shape[1])
    padded = padded_2(permeability, (("gx", 0), ("gy", 1)), margin + 1)
    weights = tuple((to_wide(field, count_x, count_y, block) for field in couplings(padded)))
    inside = (support > 0).transpose(0, 2, 1, 3)
    current = basis.transpose(0, 2, 1, 3)
    for step in range(ITERS):
        current = smooth(current, inside, *weights)
        partial_value = from_wide(current, block)
        span = 2 * margin
        lower_in = send_first(partial_value[-span:], 1)
        upper_in = send_first(partial_value[:span], -1)
        along = add_ends(partial_value, lower_in, upper_in, span, 0)
        lower_in = send_second(along[:, -span:], 1)
        upper_in = send_second(along[:, :span], -1)
        summed = add_ends(along, lower_in, upper_in, span, 1)
        summed = jnp.where(summed > 0, summed, 1.0)
        current = current / to_wide(summed, count_x, count_y, block)
    return current.transpose(0, 2, 1, 3)


def solution(mesh):
    placed = (P("gx", "gy"), P("gx", "gy", None, None), P("gx", "gy", None, None))
    return jax.shard_map(
        local, mesh=mesh, in_specs=placed, out_specs=P("gx", "gy", None, None), check_vma=False
    )
```

profile of v0, /device:TPU:4, one launch (start us, length us, event | category | flops | bytes accessed | tf_op | source)
XLA Modules:
  0.0 179.8 jit_solution(8882911816318784023)
XLA Ops:
  1.7 2.8 %collective-permute-start.1 = (f32[65,256]{0,1:T(8,128)S(1)}, f32[65,256]{0,1:T(8,128)S(1)}, u32[]{:S(2)}, u32[]{:S(2)}) collective-permute-start(f32[65,256]{0,1:T(8,128)S(1)} %get-tuple-element.67), channel_id=1, source_target_pairs={{4,0},{8,4},{12,8},{16,12},{20,16},{24,20},{28,24},{5,1},{9,5},{13... | collective-permute-start | bytes 199688 | tf_op jit(solution)/shard_map/ppermute | solution.py:27
  6.4 5.5 %copy.5 = f32[8,2,256,256]{2,0,3,1:T(8,128)} copy(f32[8,2,256,256]{3,2,1,0:T(8,128)} %param.4) | data formatting | bytes 8388608 | tf_op args[1]
  11.9 7.9 %fusion.7 = (f32[8,255,2,256]{1,0,3,2:T(8,128)}, f32[8,255,2,256]{1,0,3,2:T(8,128)}) fusion(f32[8,256,2,256]{1,0,3,2:T(8,128)} %bitcast.109), kind=kLoop, calls=%fused_computation.74 | loop fusion | bytes 16711680 | tf_op jit(solution)/shard_map/slice | solution.py:67
  19.8 5.6 %copy.4 = s32[8,2,256,256]{2,0,3,1:T(8,128)} copy(s32[8,2,256,256]{3,2,1,0:T(8,128)} %param.5) | data formatting | bytes 8388608 | tf_op args[2]
  26.3 3.5 %collective-permute-start.2 = (f32[1154,65]{0,1:T(8,128)S(1)}, f32[1154,65]{0,1:T(8,128)S(1)}, u32[]{:S(2)}, u32[]{:S(2)}) collective-permute-start(f32[1154,65]{0,1:T(8,128)S(1)} %get-tuple-element.65), channel_id=1, source_target_pairs={{0,1},{1,2},{2,3},{4,5},{5,6},{6,7},{8,9},{9,10},{10,11},{12,13},{... | collective-permute-start | bytes 900128 | tf_op jit(solution)/shard_map/ppermute | solution.py:26
  31.3 7.2 %fusion.8 = (f32[8,256,2,255]{1,0,3,2:T(8,128)}, f32[8,256,2,255]{1,0,3,2:T(8,128)}) fusion(f32[8,256,2,256]{1,0,3,2:T(8,128)} %bitcast.110), kind=kLoop, calls=%fused_computation.75 | loop fusion | bytes 16711680 | tf_op jit(solution)/shard_map/slice | solution.py:69
  38.5 4.1 %collective-permute-done.3 = f32[1154,65]{0,1:T(8,128)S(1)} collective-permute-done((f32[1154,65]{0,1:T(8,128)S(1)}, f32[1154,65]{0,1:T(8,128)S(1)}, u32[]{:S(2)}, u32[]{:S(2)}) %collective-permute-start.3) | collective-permute-done | bytes 300072 | tf_op jit(solution)/shard_map/ppermute | solution.py:27
  56.5 2.8 %constant_dynamic-update-slice_fusion.6 = f32[8,256,3,128]{1,0,3,2:T(8,128)S(1)} fusion(f32[8,256,3,128]{1,0,3,2:T(8,128)S(1)} %constant_dynamic-update-slice_fusion.7, f32[8,128,3,128]{1,0,3,2:T(8,128)} %bitcast.114), kind=kLoop, calls=%fused_computation.58 | loop fusion | bytes 3145728 | tf_op jit(solution)/shard_map/concatenate | solution.py:34
  62.3 6.5 %fusion.13 = (f32[8,256,2,128]{1,0,3,2:T(8,128)S(1)}, f32[8,256,2,128]{1,0,3,2:T(8,128)}, f32[8,256,2,128]{1,0,3,2:T(8,128)}, f32[8,256,2,128]{1,0,3,2:T(8,128)}) fusion(f32[8,256,3,128]{1,0,3,2:T(8,128)} %constant_dynamic-update-slice_fusion.4, f32[8,256,3,128]{1,0,3,2:T(8,128)} %copy-done.9), kind=kLoop, calls=%fused_computation.80 | loop fusion | bytes 16777216 | tf_op jit(solution)/shard_map/slice | solution.py:35
  68.9 11.1 %add_select_fusion.1 = (f32[8,256,2,256]{1,0,3,2:T(8,128)S(1)}, pred[8,2,256,256]{2,0,3,1:T(8,128)(4,1)S(1)}) fusion(f32[8,256,2,255]{1,0,3,2:T(8,128)} %get-tuple-element.26, f32[8,256,2,255]{1,0,3,2:T(8,128)} %get-tuple-element.25, f32[8,255,2,256]{1,0,3,2:T(8,128)} %get-tuple-element.24, f32[8,255,2,256]{1,0,3,2:T(8,128)} %get-tuple-element.23, ...), kind=kLoop, calls=%fused_computation.12 | loop fusion | flops 18874368 | bytes 51314688 | tf_op jit(solution)/shard_map/jit(_where)/select_n | solution.py:72
  82.5 4.5 %collective-permute-start.5 = (f32[128,384]{0,1:T(8,128)S(1)}, f32[128,384]{0,1:T(8,128)S(1)}, u32[]{:S(2)}, u32[]{:S(2)}) collective-permute-start(f32[128,384]{0,1:T(8,128)S(1)} %bitcast.133), channel_id=1, source_target_pairs={{4,0},{8,4},{12,8},{16,12},{20,16},{24,20},{28,24},{5,1},{9,5},{13... | collective-permute-start | bytes 589832 | tf_op jit(solution)/shard_map/ppermute | solution.py:16
  90.5 3.5 %collective-permute-start.6 = (f32[1152,128]{0,1:T(8,128)S(1)}, f32[1152,128]{0,1:T(8,128)S(1)}, u32[]{:S(2)}, u32[]{:S(2)}) collective-permute-start(f32[1152,128]{0,1:T(8,128)S(1)} %get-tuple-element.61), channel_id=1, source_target_pairs={{0,1},{1,2},{2,3},{4,5},{5,6},{6,7},{8,9},{9,10},{10,11},{12,13},{... | collective-permute-start | bytes 1769480 | tf_op jit(solution)/shard_map/ppermute | solution.py:16
  95.3 10.5 %collective-permute-done.6 = f32[1152,128]{0,1:T(8,128)S(1)} collective-permute-done((f32[1152,128]{0,1:T(8,128)S(1)}, f32[1152,128]{0,1:T(8,128)S(1)}, u32[]{:S(2)}, u32[]{:S(2)}) %collective-permute-start.6) | collective-permute-done | bytes 589856 | tf_op jit(solution)/shard_map/ppermute | solution.py:16
  105.8 4.1 %collective-permute-done.7 = f32[1152,128]{0,1:T(8,128)S(1)} collective-permute-done((f32[1152,128]{0,1:T(8,128)S(1)}, f32[1152,128]{0,1:T(8,128)S(1)}, u32[]{:S(2)}, u32[]{:S(2)}) %collective-permute-start.7) | collective-permute-done | bytes 589856 | tf_op jit(solution)/shard_map/ppermute | solution.py:16
  112.4 4.2 %fusion.5 = (f32[8,256,2,255]{1,0,3,2:T(8,128)}, f32[8,256,2,255]{1,0,3,2:T(8,128)}) fusion(f32[8,256,2,256]{1,0,3,2:T(8,128)S(1)} %maximum_divide_fusion), kind=kLoop, calls=%fused_computation.72 | loop fusion | bytes 16711680 | tf_op jit(solution)/shard_map/slice | solution.py:69
  116.9 4.7 %fusion.4 = (f32[8,255,2,256]{1,0,3,2:T(8,128)}, f32[8,255,2,256]{1,0,3,2:T(8,128)}) fusion(f32[8,256,2,256]{1,0,3,2:T(8,128)S(1)} %maximum_divide_fusion), kind=kLoop, calls=%fused_computation.71 | loop fusion | bytes 16711680 | tf_op jit(solution)/shard_map/slice | solution.py:67
  121.6 16.0 %add_select_fusion = f32[8,256,2,256]{1,0,3,2:T(8,128)} fusion(f32[8,256,2,255]{1,0,3,2:T(8,128)} %get-tuple-element.16, f32[8,256,2,255]{1,0,3,2:T(8,128)} %get-tuple-element.15, f32[8,255,2,256]{1,0,3,2:T(8,128)} %get-tuple-element.14, f32[8,255,2,256]{1,0,3,2:T(8,128)} %get-tuple-element.13, f32[8,256,2,256]{1,0,3,2:T(8,128)} %copy-done, ...), kind=kLoop, calls=%fused_computation.11 | loop fusion | flops 17825792 | bytes 47120384 | tf_op jit(solution)/shard_map/jit(_where)/select_n | solution.py:72
  137.6 2.5 %fusion.3 = (f32[8,128,2,128]{1,0,3,2:T(8,128)S(1)}, f32[8,128,2,128]{1,0,3,2:T(8,128)S(1)}, f32[8,128,2,128]{1,0,3,2:T(8,128)S(1)}, f32[8,128,2,128]{1,0,3,2:T(8,128)S(1)}) fusion(f32[8,256,2,256]{1,0,3,2:T(8,128)} %add_select_fusion), kind=kLoop, calls=%fused_computation.70 | loop fusion | bytes 8388608 | tf_op jit(solution)/shard_map/slice | solution.py:41
  142.4 4.5 %collective-permute-start.9 = (f32[128,384]{0,1:T(8,128)S(1)}, f32[128,384]{0,1:T(8,128)S(1)}, u32[]{:S(2)}, u32[]{:S(2)}) collective-permute-start(f32[128,384]{0,1:T(8,128)S(1)} %bitcast.135), channel_id=1, source_target_pairs={{4,0},{8,4},{12,8},{16,12},{20,16},{24,20},{28,24},{5,1},{9,5},{13... | collective-permute-start | bytes 589832 | tf_op jit(solution)/shard_map/ppermute | solution.py:16
  150.3 3.5 %collective-permute-start.10 = (f32[1152,128]{0,1:T(8,128)S(1)}, f32[1152,128]{0,1:T(8,128)S(1)}, u32[]{:S(2)}, u32[]{:S(2)}) collective-permute-start(f32[1152,128]{0,1:T(8,128)S(1)} %get-tuple-element.54), channel_id=1, source_target_pairs={{0,1},{1,2},{2,3},{4,5},{5,6},{6,7},{8,9},{9,10},{10,11},{12,13},{... | collective-permute-start | bytes 1769480 | tf_op jit(solution)/shard_map/ppermute | solution.py:16
  155.4 8.7 %collective-permute-done.10 = f32[1152,128]{0,1:T(8,128)S(1)} collective-permute-done((f32[1152,128]{0,1:T(8,128)S(1)}, f32[1152,128]{0,1:T(8,128)S(1)}, u32[]{:S(2)}, u32[]{:S(2)}) %collective-permute-start.10) | collective-permute-done | bytes 589856 | tf_op jit(solution)/shard_map/ppermute | solution.py:16
  164.1 4.1 %collective-permute-done.11 = f32[1152,128]{0,1:T(8,128)S(1)} collective-permute-done((f32[1152,128]{0,1:T(8,128)S(1)}, f32[1152,128]{0,1:T(8,128)S(1)}, u32[]{:S(2)}, u32[]{:S(2)}) %collective-permute-start.11) | collective-permute-done | bytes 589856 | tf_op jit(solution)/shard_map/ppermute | solution.py:16
  172.0 2.5 %fusion = f32[8,2,256,256]{2,0,3,1:T(8,128)} fusion(f32[8,256,2,256]{1,0,3,2:T(8,128)S(1)} %copy-done.2, f32[8,256,2,128]{1,0,3,2:T(8,128)S(1)} %get-tuple-element.28, f32[8,256,2,128]{1,0,3,2:T(8,128)S(1)} %get-tuple-element.27), kind=kLoop, calls=%fused_computation.10 | loop fusion | flops 2097152 | bytes 12582912 | tf_op jit(solution)/shard_map/transpose | solution.py:116
  174.6 5.2 %copy.9 = f32[8,2,256,256]{3,2,1,0:T(8,128)} copy(f32[8,2,256,256]{2,0,3,1:T(8,128)} %fusion) | data formatting | bytes 8388608 | tf_op jit(solution)/shard_map/transpose | solution.py:116
  (99 shorter events, 43.4 us)
Async XLA Ops:
  1.7 23.7 %collective-permute-start.1 = (f32[65,256]{0,1:T(8,128)S(1)}, f32[65,256]{0,1:T(8,128)S(1)}, u32[]{:S(2)}, u32[]{:S(2)}) collective-permute-start(f32[65,256]{0,1:T(8,128)S(1)} %get-tuple-element.67), channel_id=1, source_target_pairs={{4,0},{8,4},{12,8},{16,12},{20,16},{24,20},{28,24},{5,1},{9,5},{13... | collective-permute-start | bytes 199688 | tf_op jit(solution)/shard_map/ppermute | solution.py:27
  4.5 21.0 %collective-permute-start = (f32[65,256]{0,1:T(8,128)S(1)}, f32[65,256]{0,1:T(8,128)S(1)}, u32[]{:S(2)}, u32[]{:S(2)}) collective-permute-start(f32[65,256]{0,1:T(8,128)S(1)} %get-tuple-element.68), channel_id=1, source_target_pairs={{0,4},{4,8},{8,12},{12,16},{16,20},{20,24},{24,28},{1,5},{5,9},{9,... | collective-permute-start | bytes 199688 | tf_op jit(solution)/shard_map/ppermute | solution.py:26
  26.3 12.2 %collective-permute-start.2 = (f32[1154,65]{0,1:T(8,128)S(1)}, f32[1154,65]{0,1:T(8,128)S(1)}, u32[]{:S(2)}, u32[]{:S(2)}) collective-permute-start(f32[1154,65]{0,1:T(8,128)S(1)} %get-tuple-element.65), channel_id=1, source_target_pairs={{0,1},{1,2},{2,3},{4,5},{5,6},{6,7},{8,9},{9,10},{10,11},{12,13},{... | collective-permute-start | bytes 900128 | tf_op jit(solution)/shard_map/ppermute | solution.py:26
  29.8 12.8 %collective-permute-start.3 = (f32[1154,65]{0,1:T(8,128)S(1)}, f32[1154,65]{0,1:T(8,128)S(1)}, u32[]{:S(2)}, u32[]{:S(2)}) collective-permute-start(f32[1154,65]{0,1:T(8,128)S(1)} %get-tuple-element.66), channel_id=1, source_target_pairs={{1,0},{2,1},{3,2},{5,4},{6,5},{7,6},{9,8},{10,9},{11,10},{13,12},{... | collective-permute-start | bytes 900128 | tf_op jit(solution)/shard_map/ppermute | solution.py:27
  48.5 20.3 %copy-start.3 = (f32[8,256,2,128]{1,0,3,2:T(8,128)}, f32[8,256,2,128]{1,0,3,2:T(8,128)S(1)}, u32[]{:S(2)}) copy-start(f32[8,256,2,128]{1,0,3,2:T(8,128)S(1)} %get-tuple-element.40) | copy-start | bytes 6291460
  56.4 12.4 %copy-start.4 = (f32[8,256,2,128]{1,0,3,2:T(8,128)}, f32[8,256,2,128]{1,0,3,2:T(8,128)S(1)}, u32[]{:S(2)}) copy-start(f32[8,256,2,128]{1,0,3,2:T(8,128)S(1)} %get-tuple-element.31) | copy-start | bytes 6291460
  56.4 12.4 %copy-start.5 = (f32[8,256,2,128]{1,0,3,2:T(8,128)}, f32[8,256,2,128]{1,0,3,2:T(8,128)S(1)}, u32[]{:S(2)}) copy-start(f32[8,256,2,128]{1,0,3,2:T(8,128)S(1)} %get-tuple-element.32) | copy-start | bytes 6291460
  56.4 12.4 %copy-start.6 = (f32[8,256,2,128]{1,0,3,2:T(8,128)}, f32[8,256,2,128]{1,0,3,2:T(8,128)S(1)}, u32[]{:S(2)}) copy-start(f32[8,256,2,128]{1,0,3,2:T(8,128)S(1)} %get-tuple-element.69) | copy-start | bytes 6291460
  56.5 12.4 %copy-start.7 = (f32[8,256,2,128]{1,0,3,2:T(8,128)}, f32[8,256,2,128]{1,0,3,2:T(8,128)S(1)}, u32[]{:S(2)}) copy-start(f32[8,256,2,128]{1,0,3,2:T(8,128)S(1)} %get-tuple-element.70) | copy-start | bytes 6291460
  56.5 4.6 %copy-start.10 = (f32[48,8,8,128]{3,2,1,0:T(8,128)S(1)}, f32[48,8,8,128]{3,2,1,0:T(8,128)}, u32[]{:S(2)}) copy-start(f32[48,8,8,128]{3,2,1,0:T(8,128)} %copy.15) | copy-start | bytes 4718596
  59.3 1.8 copy-start.9
  62.3 6.5 %copy-start.1 = (f32[8,2,256,256]{2,0,3,1:T(8,128)S(1)}, f32[8,2,256,256]{2,0,3,1:T(8,128)}, u32[]{:S(2)}) copy-start(f32[8,2,256,256]{2,0,3,1:T(8,128)} %copy.5) | copy-start | bytes 12582916
  68.8 11.1 %copy-start.8 = (f32[8,256,2,128]{1,0,3,2:T(8,128)}, f32[8,256,2,128]{1,0,3,2:T(8,128)S(1)}, u32[]{:S(2)}) copy-start(f32[8,256,2,128]{1,0,3,2:T(8,128)S(1)} %get-tuple-element.35) | copy-start | bytes 6291460
  80.6 7.9 %collective-permute-start.4 = (f32[128,384]{0,1:T(8,128)S(1)}, f32[128,384]{0,1:T(8,128)S(1)}, u32[]{:S(2)}, u32[]{:S(2)}) collective-permute-start(f32[128,384]{0,1:T(8,128)S(1)} %bitcast.129), channel_id=1, source_target_pairs={{0,4},{4,8},{8,12},{12,16},{16,20},{20,24},{24,28},{1,5},{5,9},{9,... | collective-permute-start | bytes 589832 | tf_op jit(solution)/shard_map/ppermute | solution.py:16
  82.5 7.7 %collective-permute-start.5 = (f32[128,384]{0,1:T(8,128)S(1)}, f32[128,384]{0,1:T(8,128)S(1)}, u32[]{:S(2)}, u32[]{:S(2)}) collective-permute-start(f32[128,384]{0,1:T(8,128)S(1)} %bitcast.133), channel_id=1, source_target_pairs={{4,0},{8,4},{12,8},{16,12},{20,16},{24,20},{28,24},{5,1},{9,5},{13... | collective-permute-start | bytes 589832 | tf_op jit(solution)/shard_map/ppermute | solution.py:16
  90.5 15.4 %collective-permute-start.6 = (f32[1152,128]{0,1:T(8,128)S(1)}, f32[1152,128]{0,1:T(8,128)S(1)}, u32[]{:S(2)}, u32[]{:S(2)}) collective-permute-start(f32[1152,128]{0,1:T(8,128)S(1)} %get-tuple-element.61), channel_id=1, source_target_pairs={{0,1},{1,2},{2,3},{4,5},{5,6},{6,7},{8,9},{9,10},{10,11},{12,13},{... | collective-permute-start | bytes 1769480 | tf_op jit(solution)/shard_map/ppermute | solution.py:16
  94.0 16.0 %collective-permute-start.7 = (f32[1152,128]{0,1:T(8,128)S(1)}, f32[1152,128]{0,1:T(8,128)S(1)}, u32[]{:S(2)}, u32[]{:S(2)}) collective-permute-start(f32[1152,128]{0,1:T(8,128)S(1)} %get-tuple-element.62), channel_id=1, source_target_pairs={{1,0},{2,1},{3,2},{5,4},{6,5},{7,6},{9,8},{10,9},{11,10},{13,12},{... | collective-permute-start | bytes 1769480 | tf_op jit(solution)/shard_map/ppermute | solution.py:16
  112.4 4.5 %copy-start = (f32[8,256,2,256]{1,0,3,2:T(8,128)}, f32[8,256,2,256]{1,0,3,2:T(8,128)S(1)}, u32[]{:S(2)}) copy-start(f32[8,256,2,256]{1,0,3,2:T(8,128)S(1)} %maximum_divide_fusion) | copy-start | bytes 12582916
  140.5 8.5 %collective-permute-start.8 = (f32[128,384]{0,1:T(8,128)S(1)}, f32[128,384]{0,1:T(8,128)S(1)}, u32[]{:S(2)}, u32[]{:S(2)}) collective-permute-start(f32[128,384]{0,1:T(8,128)S(1)} %bitcast.131), channel_id=1, source_target_pairs={{0,4},{4,8},{8,12},{12,16},{16,20},{20,24},{24,28},{1,5},{5,9},{9,... | collective-permute-start | bytes 589832 | tf_op jit(solution)/shard_map/ppermute | solution.py:16
  142.4 7.7 %collective-permute-start.9 = (f32[128,384]{0,1:T(8,128)S(1)}, f32[128,384]{0,1:T(8,128)S(1)}, u32[]{:S(2)}, u32[]{:S(2)}) collective-permute-start(f32[128,384]{0,1:T(8,128)S(1)} %bitcast.135), channel_id=1, source_target_pairs={{4,0},{8,4},{12,8},{16,12},{20,16},{24,20},{28,24},{5,1},{9,5},{13... | collective-permute-start | bytes 589832 | tf_op jit(solution)/shard_map/ppermute | solution.py:16
  150.3 13.8 %collective-permute-start.10 = (f32[1152,128]{0,1:T(8,128)S(1)}, f32[1152,128]{0,1:T(8,128)S(1)}, u32[]{:S(2)}, u32[]{:S(2)}) collective-permute-start(f32[1152,128]{0,1:T(8,128)S(1)} %get-tuple-element.54), channel_id=1, source_target_pairs={{0,1},{1,2},{2,3},{4,5},{5,6},{6,7},{8,9},{9,10},{10,11},{12,13},{... | collective-permute-start | bytes 1769480 | tf_op jit(solution)/shard_map/ppermute | solution.py:16
  153.8 14.4 %collective-permute-start.11 = (f32[1152,128]{0,1:T(8,128)S(1)}, f32[1152,128]{0,1:T(8,128)S(1)}, u32[]{:S(2)}, u32[]{:S(2)}) collective-permute-start(f32[1152,128]{0,1:T(8,128)S(1)} %get-tuple-element.55), channel_id=1, source_target_pairs={{1,0},{2,1},{3,2},{5,4},{6,5},{7,6},{9,8},{10,9},{11,10},{13,12},{... | collective-permute-start | bytes 1769480 | tf_op jit(solution)/shard_map/ppermute | solution.py:16
  169.8 2.2 %copy-start.2 = (f32[8,256,2,256]{1,0,3,2:T(8,128)S(1)}, f32[8,256,2,256]{1,0,3,2:T(8,128)}, u32[]{:S(2)}) copy-start(f32[8,256,2,256]{1,0,3,2:T(8,128)} %add_select_fusion) | copy-start | bytes 12582916
where the time goes:
time: 183 us; the launch traced here: 180 us
  local copies, waits for them, and re-layouts  74.8 us (41%)
  waiting for transfers between devices  36.8 us (20%)
  other arithmetic  35.1 us (19%)
  starting transfers between devices  32.4 us (18%)
    ppermute x8, waiting for transfers between devices, shifted(): return lax.ppermute(block, axis, route)  32.7 us
    unnamed x53, local copies, waits for them, and re-layouts  28.7 us
    select_n x2, other arithmetic, smooth(): jnp.where(inside, (1.0 - relaxation) * basis + relaxation * coupled / dia...  27.1 us
    ppermute x8, starting transfers between devices, shifted(): return lax.ppermute(block, axis, route)  22.8 us
    slice x2, local copies, waits for them, and re-layouts, smooth(): from_east = jnp.pad(basis[:, 1:], (none, (0, 1), none, none))  12.6 us
    slice x2, local copies, waits for them, and re-layouts, smooth(): from_north = jnp.pad(basis[:, :, :, 1:], (none, none, none, (0, 1)))  11.4 us
    slice x5, local copies, waits for them, and re-layouts, to_wide(): return jnp.concatenate([rows[:, :, :-1], rows[:, :, 1:]], axis=3)  8.19 us
    ppermute x2, starting transfers between devices, padded_2(): before = lax.ppermute(last, axis, up)  5.42 us
  transfers between devices with their start and end apart: 12, of which 9 were waited for; matrix products, arithmetic and copies ran while one was open for 15% of the time, Pallas kernels for 0%

commit v1 on v0

v1 whole, which is shorter than its diff:
```python
import jax
import jax.numpy as jnp
from jax import lax
from jax.experimental import pallas as pl
from jax.experimental.pallas import tpu as pltpu
from jax.sharding import PartitionSpec as P

ITERS = 2
MESH = pl.DeviceIdType.MESH
relaxation = 2.0 / 3.0
PAD = 8
CH = 32


def padded_2(shard, sides, width):
    for axis, dim in sides:
        devices, length = (lax.axis_size(axis), shard.shape[dim])
        up = [(i, (i + 1) % devices) for i in range(devices - 1)]
        down = [(j, i) for i, j in up]
        last = lax.slice_in_dim(shard, length - width, length, axis=dim)
        initial = lax.slice_in_dim(shard, 0, width, axis=dim)
        before = lax.ppermute(last, axis, up)
        after = lax.ppermute(initial, axis, down)
        shard = jnp.concatenate([before, shard, after], axis=dim)
    return shard


def harmonic(left, right):
    summed = left + right
    inside = summed > 0
    return jnp.where(inside, 2.0 * left * right / jnp.where(inside, summed, 1.0), 0.0)


def scaled_couplings(padded):
    faces_x = harmonic(padded[:-1, 1:-1], padded[1:, 1:-1])
    faces_y = harmonic(padded[1:-1, :-1], padded[1:-1, 1:])
    east = faces_x[1:]
    west = faces_x[:-1]
    north = faces_y[:, 1:]
    south = faces_y[:, :-1]
    diagonal = east + west + north + south
    scale = relaxation / jnp.where(diagonal > 0, diagonal, 1.0)
    return (east * scale, west * scale, north * scale, south * scale)


def make_kernel(nx, ny, size_x, size_y, half):
    full = 2 * half
    last = nx
    strips = ny + 1

    def kernel(*refs):
        (we_h, ww_h, wn_h, ws_h, basis_h, out_h,
         a, b, d, w, s, inv, rz, rx,
         a_sem, w_sem, o_sem, zs_sem, zr_sem, xs_sem, xr_sem) = refs
        gx, gy = lax.axis_index("gx"), lax.axis_index("gy")
        has_up, has_down = gx > 0, gx < size_x - 1
        has_left, has_right = gy > 0, gy < size_y - 1
        up, down = (gx - 1, gy), (gx + 1, gy)
        left, right = (gx, gy - 1), (gx, gy + 1)
        z_sides = ((0, has_left, left), (1, has_right, right))
        x_sides = ((0, has_up, up), (1, has_down, down))

        def row1(k):
            return jnp.where(k == 0, 0, jnp.where(k == 1, nx - 1, k - 1))

        def a_copy(i):
            return pltpu.make_async_copy(basis_h.at[i], a.at[i, :, pl.ds(PAD, full), :], a_sem.at[i])

        def w_copy(n, rb):
            src = (we_h, ww_h, wn_h, ws_h)[n]
            return pltpu.make_async_copy(
                src.at[pl.ds(pl.multiple_of(rb * half, half), half), :], w.at[n, rb], w_sem.at[n, rb])

        def o_copy(i):
            return pltpu.make_async_copy(a.at[i, :, pl.ds(PAD, full), :], out_h.at[i], o_sem.at[i])

        def z_copy(it, side, target, rb):
            strip = 0 if side == 0 else strips - 1
            return pltpu.make_async_remote_copy(
                src_ref=s.at[it, rb, strip], dst_ref=rz.at[it, 1 - side, rb],
                send_sem=zs_sem.at[it, side, rb], recv_sem=zr_sem.at[it, 1 - side, rb],
                device_id=target, device_id_type=MESH)

        def z_arrival(it, side, target, rb):
            return pltpu.make_async_remote_copy(
                src_ref=s.at[it, rb, 0], dst_ref=rz.at[it, side, rb],
                send_sem=zs_sem.at[it, side, rb], recv_sem=zr_sem.at[it, side, rb],
                device_id=target, device_id_type=MESH)

        def x_copy(it, side, target):
            rb = 0 if side == 0 else last
            return pltpu.make_async_remote_copy(
                src_ref=s.at[it, rb], dst_ref=rx.at[it, 1 - side],
                send_sem=xs_sem.at[it, side], recv_sem=xr_sem.at[it, 1 - side],
                device_id=target, device_id_type=MESH)

        def x_arrival(it, side, target):
            return pltpu.make_async_remote_copy(
                src_ref=s.at[it, 0], dst_ref=rx.at[it, side],
                send_sem=xs_sem.at[it, side], recv_sem=xr_sem.at[it, side],
                device_id=target, device_id_type=MESH)

        barrier = pltpu.get_barrier_semaphore()
        for _, has, target in z_sides + x_sides:
            @pl.when(has)
            def _():
                pl.semaphore_signal(barrier, inc=1, device_id=target, device_id_type=MESH)

        @pl.loop(0, nx)
        def _(k):
            a_copy(row1(k)).start()

        @pl.loop(0, nx + 1)
        def _(rb):
            for n in range(4):
                w_copy(n, rb).start()

        edge = jnp.zeros((PAD, full), jnp.float32)
        blank = jnp.zeros((half, half), jnp.float32)

        @pl.loop(0, nx)
        def _(i):
            for j in range(ny):
                a[i, j, 0:PAD, :] = edge
                a[i, j, PAD + full:, :] = edge
                b[i + 1, j, 0:PAD, :] = edge
                b[i + 1, j, PAD + full:, :] = edge

        for buf in (b, d):
            for j in range(ny):
                for r in range(0, full, half):
                    buf[0, j, PAD + r:PAD + r + half, :] = jnp.zeros((half, full), jnp.float32)
                    buf[nx + 1, j, PAD + r:PAD + r + half, :] = jnp.zeros((half, full), jnp.float32)

        for side, has, _t in z_sides:
            @pl.when(jnp.logical_not(has))
            def _():
                @pl.loop(0, nx + 1)
                def _(rb):
                    for it in range(ITERS):
                        rz[it, side, rb] = blank

        lanes = lax.broadcasted_iota(jnp.int32, (CH, full), 1)
        not_last, not_first = lanes < full - 1, lanes > 0

        def smooth_row(i, first):
            for j in range(ny):
                for r in range(0, full, CH):
                    lo = PAD + r
                    rb = i + r // half
                    q = r % half

                    def load(shift):
                        if first:
                            return a[i, j, lo + shift:lo + shift + CH, :]
                        return b[i + 1, j, lo + shift:lo + shift + CH, :]

                    def weight(n):
                        return w[n, rb, q:q + CH, j * half:j * half + full]

                    x = load(0)
                    ahead = jnp.where(not_last, pltpu.roll(x, full - 1, 1), 0.0)
                    behind = jnp.where(not_first, pltpu.roll(x, 1, 1), 0.0)
                    new = (1.0 - relaxation) * x + weight(0) * load(1) + weight(1) * load(-1)
                    new = new + weight(2) * ahead + weight(3) * behind
                    mask = x if first else a[i, j, lo:lo + CH, :]
                    new = jnp.where(mask > 0, new, 0.0)
                    if first:
                        b[i + 1, j, lo:lo + CH, :] = new
                    else:
                        d[i + 1, j, lo:lo + CH, :] = new

        def partial(it, rb):
            src = b if it == 0 else d
            for c in range(strips):
                for r in range(0, half, CH):
                    total = None
                    for j, lane in ((c - 1, half), (c, 0)):
                        if 0 <= j < ny:
                            low = src[rb, j, PAD + half + r:PAD + half + r + CH, lane:lane + half]
                            high = src[rb + 1, j, PAD + r:PAD + r + CH, lane:lane + half]
                            term = low + high
                            total = term if total is None else total + term
                    s[it, rb, c, r:r + CH, :] = total

        def z_send(it, rb):
            for side, has, target in z_sides:
                @pl.when(has)
                def _():
                    z_copy(it, side, target, rb).start()

        def invert(it, rb):
            for side, has, target in z_sides:
                @pl.when(has)
                def _():
                    z_arrival(it, side, target, rb).wait_recv()
            for c in range(strips):
                for r in range(0, half, CH):
                    total = s[it, rb, c, r:r + CH, :]
                    if c == 0:
                        total = total + rz[it, 0, rb, r:r + CH, :]
                    if c == strips - 1:
                        total = total + rz[it, 1, rb, r:r + CH, :]
                    inv[rb, r:r + CH, c * half:(c + 1) * half] = 1.0 / jnp.where(total > 0, total, 1.0)

        def x_send(it, side):
            _, has, target = x_sides[side]

            @pl.when(has)
            def _():
                x_copy(it, side, target).start()

        def x_add(it, side):
            _, has, target = x_sides[side]
            rb = 0 if side == 0 else last

            @pl.when(has)
            def _():
                x_copy(it, side, target).wait_send()
                x_arrival(it, side, target).wait_recv()
                for c in range(strips):
                    s[it, rb, c] = s[it, rb, c] + rx[it, side, c]

        def normalise(i, src, dst):
            for j in range(ny):
                for r in range(0, full, CH):
                    rb = i + r // half
                    q = r % half
                    lo = PAD + r
                    value = src[i + 1, j, lo:lo + CH, :] * inv[rb, q:q + CH, j * half:j * half + full]
                    if dst is None:
                        src[i + 1, j, lo:lo + CH, :] = value
                    else:
                        dst[i, j, lo:lo + CH, :] = value

        def w_wait(rb):
            for n in range(4):
                w_copy(n, rb).wait()

        peers = sum(jnp.where(has, 1, 0) for _, has, _t in z_sides + x_sides)
        pl.semaphore_wait(barrier, peers)

        @pl.loop(0, nx)
        def _(k):
            i = row1(k)
            a_copy(i).wait()

            @pl.when(k == 0)
            def _():
                w_wait(0)
                w_wait(1)

            @pl.when(k == 1)
            def _():
                w_wait(nx - 1)
                w_wait(nx)

            @pl.when((k >= 2) & (k < nx - 1))
            def _():
                w_wait(i + 1)

            smooth_row(i, True)

            @pl.when(k == 0)
            def _():
                partial(0, 0)
                x_send(0, 0)

            @pl.when(k == 1)
            def _():
                partial(0, last)
                x_send(0, 1)

            @pl.when(k >= 2)
            def _():
                partial(0, i)
                z_send(0, i)

            @pl.when(k == nx - 1)
            def _():
                partial(0, nx - 1)
                z_send(0, nx - 1)

        x_add(0, 0)
        z_send(0, 0)
        x_add(0, 1)
        z_send(0, last)

        invert(0, 1)

        @pl.loop(0, nx)
        def _(k):
            i = jnp.where(k < nx - 2, k + 1, jnp.where(k == nx - 2, 0, nx - 1))
            invert(0, jnp.where(k < nx - 2, k + 2, jnp.where(k == nx - 2, 0, nx)))
            normalise(i, b, None)
            smooth_row(i, False)

            @pl.when((k >= 1) & (k < nx - 2))
            def _():
                partial(1, i)
                z_send(1, i)

            @pl.when(k >= nx - 2)
            def _():
                rb = jnp.where(k == nx - 2, 1, nx - 1)
                partial(1, rb)
                z_send(1, rb)
                partial(1, jnp.where(k == nx - 2, 0, nx))

            @pl.when(k == nx - 2)
            def _():
                x_send(1, 0)

            @pl.when(k == nx - 1)
            def _():
                x_send(1, 1)

        x_add(1, 0)
        z_send(1, 0)
        x_add(1, 1)
        z_send(1, last)

        invert(1, 2)

        @pl.loop(0, nx)
        def _(k):
            n = nx - 4
            i = jnp.where(k < n, k + 2, jnp.where(k == n, 1, jnp.where(
                k == n + 1, nx - 2, jnp.where(k == n + 2, 0, nx - 1))))
            rb = jnp.where(k < n, k + 3, jnp.where(k == n, 1, jnp.where(
                k == n + 1, nx - 1, jnp.where(k == n + 2, 0, nx))))
            invert(1, rb)
            normalise(i, d, a)
            o_copy(i).start()

        @pl.loop(0, nx)
        def _(i):
            o_copy(i).wait()

        for side, has, target in z_sides:
            @pl.when(has)
            def _():
                @pl.loop(0, nx + 1)
                def _(rb):
                    for it in range(ITERS):
                        z_copy(it, side, target, rb).wait_send()

    return kernel


def local(permeability, basis, support):
    nx, ny, full, _ = basis.shape
    half = full // 2
    size_x, size_y = lax.axis_size("gx"), lax.axis_size("gy")
    padded = padded_2(permeability, (("gx", 0), ("gy", 1)), half // 2 + 1)
    weights = scaled_couplings(padded)
    f32 = jnp.float32
    strips = ny + 1
    scratch = [
        pltpu.VMEM((nx, ny, full + 2 * PAD, full), f32),
        pltpu.VMEM((nx + 2, ny, full + 2 * PAD, full), f32),
        pltpu.VMEM((nx + 2, ny, full + 2 * PAD, full), f32),
        pltpu.VMEM((4, nx + 1, half, strips * half), f32),
        pltpu.VMEM((ITERS, nx + 1, strips, half, half), f32),
        pltpu.VMEM((nx + 1, half, strips * half), f32),
        pltpu.VMEM((ITERS, 2, nx + 1, half, half), f32),
        pltpu.VMEM((ITERS, 2, strips, half, half), f32),
        pltpu.SemaphoreType.DMA((nx,)),
        pltpu.SemaphoreType.DMA((4, nx + 1)),
        pltpu.SemaphoreType.DMA((nx,)),
        pltpu.SemaphoreType.DMA((ITERS, 2, nx + 1)),
        pltpu.SemaphoreType.DMA((ITERS, 2, nx + 1)),
        pltpu.SemaphoreType.DMA((ITERS, 2)),
        pltpu.SemaphoreType.DMA((ITERS, 2)),
    ]
    return pl.pallas_call(
        make_kernel(nx, ny, size_x, size_y, half),
        out_shape=jax.ShapeDtypeStruct(basis.shape, f32),
        in_specs=[pl.BlockSpec(memory_space=pl.ANY)] * 5,
        out_specs=pl.BlockSpec(memory_space=pl.ANY),
        scratch_shapes=scratch,
        compiler_params=pltpu.CompilerParams(
            collective_id=0, has_side_effects=True, vmem_limit_bytes=48 * 1024 * 1024),
        name="smoothing",
    )(*weights, basis)


def solution(mesh):
    placed = (P("gx", "gy"), P("gx", "gy", None, None), P("gx", "gy", None, None))
    return jax.shard_map(
        local, mesh=mesh, in_specs=placed, out_specs=P("gx", "gy", None, None), check_vma=False
    )
```

time: 183 us -> 76.2 us (0.42)
  the two profiles are of different devices: /device:TPU:4 before, /device:TPU:0 now
where the time goes in v1:
time: 76.2 us; the launch traced here: 75.8 us
  Pallas kernels  40.2 us (53%)
  starting transfers between devices  11.2 us (15%)
  local copies, waits for them, and re-layouts  9.96 us (13%)
  waiting for transfers between devices  8.78 us (12%)
  other arithmetic  5.64 us (7%)
    pallas_call x1, Pallas kernels, local(): pl.pallas_call(make_kernel(nx, ny, size_x, size_y, half), out_shape=jax.S...  40.2 us
    ppermute x2, starting transfers between devices, padded_2(): before = lax.ppermute(last, axis, up)  8.64 us
    ppermute x2, waiting for transfers between devices, padded_2(): after = lax.ppermute(initial, axis, down)  6.16 us
    unnamed x1, local copies, waits for them, and re-layouts  4.6 us
    concatenate x1, local copies, waits for them, and re-layouts, padded_2(): shard = jnp.concatenate([before, shard, after], axis=dim)  3.23 us
    ppermute x2, waiting for transfers between devices, padded_2(): before = lax.ppermute(last, axis, up)  2.61 us
    mul x2, other arithmetic, scaled_couplings(): return (east * scale, west * scale, north * scale, south * scale)  2.61 us
    ppermute x2, starting transfers between devices, padded_2(): after = lax.ppermute(initial, axis, down)  2.58 us
  transfers between devices with their start and end apart: 4, of which 3 were waited for; matrix products, arithmetic and copies ran while one was open for 1% of the time, Pallas kernels for 0%

profile of v1, /device:TPU:0, one launch (start us, length us, event | category | flops | bytes accessed | tf_op | source)
XLA Modules:
  0.0 75.8 jit_solution(17840819284144165466)
XLA Ops:
  0.0 0.9 %fusion.5 = (f32[65,256]{1,0:T(8,128)S(1)}, f32[65,256]{1,0:T(8,128)S(1)}) fusion(f32[1024,256]{1,0:T(8,128)} %param.3), kind=kLoop, calls=%fused_computation.14 | loop fusion | bytes 266240 | tf_op jit(solution)/shard_map/slice | solution.py:21
  0.9 1.3 %collective-permute-start.1 = (f32[65,256]{1,0:T(8,128)S(1)}, f32[65,256]{1,0:T(8,128)S(1)}, u32[]{:S(2)}, u32[]{:S(2)}) collective-permute-start(f32[65,256]{1,0:T(8,128)S(1)} %get-tuple-element.12), channel_id=1, source_target_pairs={{4,0},{8,4},{12,8},{16,12},{20,16},{24,20},{28,24},{5,1},{9,5},{13... | collective-permute-start | bytes 199688 | tf_op jit(solution)/shard_map/ppermute | solution.py:23
  2.2 3.0 %collective-permute-start = (f32[65,256]{1,0:T(8,128)S(1)}, f32[65,256]{1,0:T(8,128)S(1)}, u32[]{:S(2)}, u32[]{:S(2)}) collective-permute-start(f32[65,256]{1,0:T(8,128)S(1)} %get-tuple-element.13), channel_id=1, source_target_pairs={{0,4},{4,8},{8,12},{12,16},{16,20},{20,24},{24,28},{1,5},{5,9},{9,... | collective-permute-start | bytes 199688 | tf_op jit(solution)/shard_map/ppermute | solution.py:22
  5.3 0.0 collective-permute-done.1
  5.3 0.9 %collective-permute-done = f32[65,256]{1,0:T(8,128)S(1)} collective-permute-done((f32[65,256]{1,0:T(8,128)S(1)}, f32[65,256]{1,0:T(8,128)S(1)}, u32[]{:S(2)}, u32[]{:S(2)}) %collective-permute-start) | collective-permute-done | bytes 66592 | tf_op jit(solution)/shard_map/ppermute | solution.py:22
  6.2 3.2 %concatenate.6 = f32[1154,256]{1,0:T(8,128)S(1)} concatenate(f32[65,256]{1,0:T(8,128)S(1)} %collective-permute-done, f32[1024,256]{1,0:T(8,128)} %param.3, f32[65,256]{1,0:T(8,128)S(1)} %collective-permute-done.1), dimensions={0} | concatenate | bytes 2363392 | tf_op jit(solution)/shard_map/concatenate | solution.py:24
  9.4 0.2 fusion.4
  9.6 0.3 copy.4
  9.9 1.3 %collective-permute-start.3 = (f32[1154,65]{0,1:T(8,128)S(1)}, f32[1154,65]{0,1:T(8,128)S(1)}, u32[]{:S(2)}, u32[]{:S(2)}) collective-permute-start(f32[1154,65]{0,1:T(8,128)S(1)} %copy.4), channel_id=1, source_target_pairs={{1,0},{2,1},{3,2},{5,4},{6,5},{7,6},{9,8},{10,9},{11,10},{13,12},{... | collective-permute-start | bytes 900128 | tf_op jit(solution)/shard_map/ppermute | solution.py:23
  11.2 0.2 copy.3
  11.4 5.6 %collective-permute-start.2 = (f32[1154,65]{0,1:T(8,128)S(1)}, f32[1154,65]{0,1:T(8,128)S(1)}, u32[]{:S(2)}, u32[]{:S(2)}) collective-permute-start(f32[1154,65]{0,1:T(8,128)S(1)} %copy.3), channel_id=1, source_target_pairs={{0,1},{1,2},{2,3},{4,5},{5,6},{6,7},{8,9},{9,10},{10,11},{12,13},{... | collective-permute-start | bytes 900128 | tf_op jit(solution)/shard_map/ppermute | solution.py:22
  17.0 6.2 %collective-permute-done.3 = f32[1154,65]{0,1:T(8,128)S(1)} collective-permute-done((f32[1154,65]{0,1:T(8,128)S(1)}, f32[1154,65]{0,1:T(8,128)S(1)}, u32[]{:S(2)}, u32[]{:S(2)}) %collective-permute-start.3) | collective-permute-done | bytes 300072 | tf_op jit(solution)/shard_map/ppermute | solution.py:23
  23.2 0.2 copy.6
  23.4 1.7 %collective-permute-done.2 = f32[1154,65]{0,1:T(8,128)S(1)} collective-permute-done((f32[1154,65]{0,1:T(8,128)S(1)}, f32[1154,65]{0,1:T(8,128)S(1)}, u32[]{:S(2)}, u32[]{:S(2)}) %collective-permute-start.2) | collective-permute-done | bytes 300072 | tf_op jit(solution)/shard_map/ppermute | solution.py:22
  25.2 0.2 copy.5
  25.4 0.9 %pad_maximum_fusion = f32[1154,386]{1,0:T(8,128)S(1)} fusion(f32[1154,65]{1,0:T(8,128)S(1)} %copy.6, f32[1154,256]{1,0:T(8,128)S(1)} %concatenate.6, f32[1154,65]{1,0:T(8,128)S(1)} %copy.5), kind=kLoop, calls=%fused_computation.3 | loop fusion | flops 890888 | bytes 3563552 | tf_op jit(solution)/shard_map/concatenate | solution.py:24
  26.3 1.0 %compare_select_fusion.3 = f32[1153,384]{1,0:T(8,128)S(1)} fusion(f32[1154,386]{1,0:T(8,128)S(1)} %pad_maximum_fusion), kind=kLoop, calls=%fused_computation.5 | loop fusion | flops 3099264 | bytes 5313024 | tf_op jit(solution)/shard_map/jit(_where)/select_n | solution.py:31
  27.3 1.2 %compare_select_fusion.1 = f32[1152,385]{1,0:T(8,128)S(1)} fusion(f32[1154,386]{1,0:T(8,128)S(1)} %pad_maximum_fusion), kind=kLoop, calls=%fused_computation.1 | loop fusion | flops 3104640 | bytes 5322240 | tf_op jit(solution)/shard_map/jit(_where)/select_n | solution.py:31
  28.5 2.0 %slice_multiply_fusion = (f32[1152,384]{1,0:T(8,128)}, f32[1152,384]{1,0:T(8,128)S(1)}) fusion(f32[1152,385]{1,0:T(8,128)S(1)} %compare_select_fusion.1, f32[1153,384]{1,0:T(8,128)S(1)} %compare_select_fusion.3), kind=kLoop, calls=%fused_computation.9 | loop fusion | flops 3096576 | bytes 10616832 | tf_op jit(solution)/shard_map/mul | solution.py:43
  30.4 0.7 slice_multiply_fusion.2
  31.1 40.2 %smoothing.1 = f32[8,2,256,256]{3,2,1,0:T(8,128)} custom-call(f32[1152,384]{1,0:T(8,128)S(1)} %get-tuple-element.8.refs_0_, f32[1152,384]{1,0:T(8,128)S(1)} %get-tuple-element.7.refs_1_, f32[1152,384]{1,0:T(8,128)S(1)} %get-tuple-element.9.refs_2_, f32[1152,384]{1,0:T(8,128)} %get-tuple-element.5.refs_3_, f32[8,2,256,256]{3,2,1,0:T(8,128)} %refs_4_.1), custom_call_target="tpu_custom_call" | custom-call | tf_op jit(solution)/shard_map/smoothing/pallas_call | solution.py:376
  71.2 4.6 %copy.8 = f32[8,2,256,256]{3,2,1,0:T(8,128)} copy(f32[8,2,256,256]{3,2,1,0:T(8,128)} %smoothing.1) | data formatting | bytes 8388608
Async XLA Ops:
  0.9 4.3 %collective-permute-start.1 = (f32[65,256]{1,0:T(8,128)S(1)}, f32[65,256]{1,0:T(8,128)S(1)}, u32[]{:S(2)}, u32[]{:S(2)}) collective-permute-start(f32[65,256]{1,0:T(8,128)S(1)} %get-tuple-element.12), channel_id=1, source_target_pairs={{4,0},{8,4},{12,8},{16,12},{20,16},{24,20},{28,24},{5,1},{9,5},{13... | collective-permute-start | bytes 199688 | tf_op jit(solution)/shard_map/ppermute | solution.py:23
  2.2 3.9 %collective-permute-start = (f32[65,256]{1,0:T(8,128)S(1)}, f32[65,256]{1,0:T(8,128)S(1)}, u32[]{:S(2)}, u32[]{:S(2)}) collective-permute-start(f32[65,256]{1,0:T(8,128)S(1)} %get-tuple-element.13), channel_id=1, source_target_pairs={{0,4},{4,8},{8,12},{12,16},{16,20},{20,24},{24,28},{1,5},{5,9},{9,... | collective-permute-start | bytes 199688 | tf_op jit(solution)/shard_map/ppermute | solution.py:22
  9.9 13.3 %collective-permute-start.3 = (f32[1154,65]{0,1:T(8,128)S(1)}, f32[1154,65]{0,1:T(8,128)S(1)}, u32[]{:S(2)}, u32[]{:S(2)}) collective-permute-start(f32[1154,65]{0,1:T(8,128)S(1)} %copy.4), channel_id=1, source_target_pairs={{1,0},{2,1},{3,2},{5,4},{6,5},{7,6},{9,8},{10,9},{11,10},{13,12},{... | collective-permute-start | bytes 900128 | tf_op jit(solution)/shard_map/ppermute | solution.py:23
  11.4 13.8 %collective-permute-start.2 = (f32[1154,65]{0,1:T(8,128)S(1)}, f32[1154,65]{0,1:T(8,128)S(1)}, u32[]{:S(2)}, u32[]{:S(2)}) collective-permute-start(f32[1154,65]{0,1:T(8,128)S(1)} %copy.3), channel_id=1, source_target_pairs={{0,1},{1,2},{2,3},{4,5},{5,6},{6,7},{8,9},{9,10},{10,11},{12,13},{... | collective-permute-start | bytes 900128 | tf_op jit(solution)/shard_map/ppermute | solution.py:22

commit v2 on v1

--- a/solution.py
+++ b/solution.py
@@ -12,35 +12,34 @@
 CH = 32
 
 
-def padded_2(shard, sides, width):
-    for axis, dim in sides:
-        devices, length = (lax.axis_size(axis), shard.shape[dim])
-        up = [(i, (i + 1) % devices) for i in range(devices - 1)]
-        down = [(j, i) for i, j in up]
-        last = lax.slice_in_dim(shard, length - width, length, axis=dim)
-        initial = lax.slice_in_dim(shard, 0, width, axis=dim)
-        before = lax.ppermute(last, axis, up)
-        after = lax.ppermute(initial, axis, down)
-        shard = jnp.concatenate([before, shard, after], axis=dim)
-    return shard
-
-
 def harmonic(left, right):
-    summed = left + right
-    inside = summed > 0
-    return jnp.where(inside, 2.0 * left * right / jnp.where(inside, summed, 1.0), 0.0)
-
-
-def scaled_couplings(padded):
-    faces_x = harmonic(padded[:-1, 1:-1], padded[1:, 1:-1])
-    faces_y = harmonic(padded[1:-1, :-1], padded[1:-1, 1:])
-    east = faces_x[1:]
-    west = faces_x[:-1]
-    north = faces_y[:, 1:]
-    south = faces_y[:, :-1]
-    diagonal = east + west + north + south
-    scale = relaxation / jnp.where(diagonal > 0, diagonal, 1.0)
-    return (east * scale, west * scale, north * scale, south * scale)
+    return 2.0 * left * right / jnp.maximum(left + right, 1e-30)
+
+
+def pick(k, table):
+    value = jnp.int32(table[-1])
+    for n in range(len(table) - 2, -1, -1):
+        value = jnp.where(k == n, table[n], value)
+    return value
+
+
+def completed(rows, count):
+    done, out = set(), []
+    for i in rows:
+        done.add(i)
+        new = [rb for rb in (i, i + 1) if 0 < rb < count and rb - 1 in done and rb in done]
+        assert len(new) <= 1
+        out.append(new[0] if new else -1)
+    return out
+
+
+def needed(rows):
+    seen, out = set(), []
+    for i in rows:
+        new = [rb for rb in (i, i + 1) if rb not in seen]
+        seen.update(new)
+        out.append(new)
+    return out
 
 
 def make_kernel(nx, ny, size_x, size_y, half):
@@ -49,9 +48,10 @@
     strips = ny + 1
 
     def kernel(*refs):
-        (we_h, ww_h, wn_h, ws_h, basis_h, out_h,
-         a, b, d, w, s, inv, rz, rx,
-         a_sem, w_sem, o_sem, zs_sem, zr_sem, xs_sem, xr_sem) = refs
+        (perm_h, basis_h, out_h,
+         a, b, d, w, s, inv, rz, rx, px, pe, pk, pr, hk, hr,
+         a_sem, p_sem, o_sem, zs_sem, zr_sem, xs_sem, xr_sem,
+         ps_sem, pr_sem, hs_sem, hr_sem, rs_sem, rr_sem) = refs
         gx, gy = lax.axis_index("gx"), lax.axis_index("gy")
         has_up, has_down = gx > 0, gx < size_x - 1
         has_left, has_right = gy > 0, gy < size_y - 1
@@ -60,16 +60,56 @@
         z_sides = ((0, has_left, left), (1, has_right, right))
         x_sides = ((0, has_up, up), (1, has_down, down))
 
-        def row1(k):
-            return jnp.where(k == 0, 0, jnp.where(k == 1, nx - 1, k - 1))
+        rows_1 = list(range(2, nx - 2)) + [1, nx - 2, 0, nx - 1]
+        rows_2 = list(range(3, nx - 3)) + [2, nx - 3, 1, nx - 2, 0, nx - 1]
+        need_1, need_2 = needed(rows_1), needed(rows_2)
+        ready_1, ready_2 = completed(rows_1, nx), completed(rows_2, nx)
+        halo = half // 2 + PAD
+        height = px.shape[0]
+        length = height - 2 * halo
+        hw = half // 2
 
         def a_copy(i):
             return pltpu.make_async_copy(basis_h.at[i], a.at[i, :, pl.ds(PAD, full), :], a_sem.at[i])
 
-        def w_copy(n, rb):
-            src = (we_h, ww_h, wn_h, ws_h)[n]
-            return pltpu.make_async_copy(
-                src.at[pl.ds(pl.multiple_of(rb * half, half), half), :], w.at[n, rb], w_sem.at[n, rb])
+        def row_copy(side, target):
+            src = 0 if side == 0 else length - halo
+            dst = height - halo if side == 0 else 0
+            return pltpu.make_async_remote_copy(
+                src_ref=perm_h.at[pl.ds(src, halo), :], dst_ref=px.at[pl.ds(dst, halo), :],
+                send_sem=rs_sem.at[side], recv_sem=rr_sem.at[1 - side],
+                device_id=target, device_id_type=MESH)
+
+        def row_arrival(side, target):
+            dst = 0 if side == 0 else height - halo
+            return pltpu.make_async_remote_copy(
+                src_ref=perm_h.at[pl.ds(0, halo), :], dst_ref=px.at[pl.ds(dst, halo), :],
+                send_sem=rs_sem.at[side], recv_sem=rr_sem.at[side],
+                device_id=target, device_id_type=MESH)
+
+        def pk_copy(side, target, rb):
+            return pltpu.make_async_remote_copy(
+                src_ref=pk.at[side, rb], dst_ref=pr.at[1 - side, rb],
+                send_sem=ps_sem.at[side, rb], recv_sem=pr_sem.at[1 - side, rb],
+                device_id=target, device_id_type=MESH)
+
+        def pk_arrival(side, target, rb):
+            return pltpu.make_async_remote_copy(
+                src_ref=pk.at[side, rb], dst_ref=pr.at[side, rb],
+                send_sem=ps_sem.at[side, rb], recv_sem=pr_sem.at[side, rb],
+                device_id=target, device_id_type=MESH)
+
+        def hk_copy(side, target):
+            return pltpu.make_async_remote_copy(
+                src_ref=hk, dst_ref=hr.at[1 - side],
+                send_sem=hs_sem.at[side], recv_sem=hr_sem.at[1 - side],
+                device_id=target, device_id_type=MESH)
+
+        def hk_arrival(side, target):
+            return pltpu.make_async_remote_copy(
+                src_ref=hk, dst_ref=hr.at[side],
+                send_sem=hs_sem.at[side], recv_sem=hr_sem.at[side],
+                device_id=target, device_id_type=MESH)
 
         def o_copy(i):
             return pltpu.make_async_copy(a.at[i, :, pl.ds(PAD, full), :], out_h.at[i], o_sem.at[i])
@@ -106,14 +146,12 @@
             def _():
                 pl.semaphore_signal(barrier, inc=1, device_id=target, device_id_type=MESH)
 
+        own = pltpu.make_async_copy(perm_h, px.at[pl.ds(halo, length), :], p_sem)
+        own.start()
+
         @pl.loop(0, nx)
         def _(k):
-            a_copy(row1(k)).start()
-
-        @pl.loop(0, nx + 1)
-        def _(rb):
-            for n in range(4):
-                w_copy(n, rb).start()
+            a_copy(pick(k, rows_1)).start()
 
         edge = jnp.zeros((PAD, full), jnp.float32)
         blank = jnp.zeros((half, half), jnp.float32)
@@ -139,6 +177,14 @@
                 def _(rb):
                     for it in range(ITERS):
                         rz[it, side, rb] = blank
+                    pr[side, rb] = jnp.zeros((hw + PAD, half), jnp.float32)
+                hr[side] = jnp.zeros((2, PAD, half), jnp.float32)
+
+        for side, has, _t in x_sides:
+            @pl.when(jnp.logical_not(has))
+            def _():
+                lo = 0 if side == 0 else height - halo
+                px[lo:lo + halo, :] = jnp.zeros((halo, full), jnp.float32)
 
         lanes = lax.broadcasted_iota(jnp.int32, (CH, full), 1)
         not_last, not_first = lanes < full - 1, lanes > 0
@@ -233,103 +279,195 @@
                     else:
                         dst[i, j, lo:lo + CH, :] = value
 
-        def w_wait(rb):
-            for n in range(4):
-                w_copy(n, rb).wait()
+        lane = lax.broadcasted_iota(jnp.int32, (hw, half), 1)
+        low_half = lane < hw
+        lane8 = lax.broadcasted_iota(jnp.int32, (PAD, half), 1)
+
+        def shifted_rows(lo, count):
+            return pltpu.roll(px[pl.ds(lo, count), :], hw, 1)
+
+        def pack(rb):
+            lo = pl.multiple_of(rb * half + PAD, PAD)
+            first = shifted_rows(lo, hw)
+            second = shifted_rows(lo + hw, hw)
+            m0, m1 = first[:, :half], second[:, :half]
+            pk[1, rb, 0:hw, :] = jnp.where(low_half, m0, pltpu.roll(m1, hw, 1))
+            pk[0, rb, 0:hw, :] = jnp.where(low_half, pltpu.roll(m0, hw, 1), m1)
+            to_left = jnp.zeros((PAD, half), jnp.float32)
+            to_right = to_left
+            for k in range(half // PAD):
+                part = first if k * PAD < hw else second
+                q = k * PAD % hw
+                e = part[q:q + PAD, half:]
+                here = lane8 == k
+                to_left = jnp.where(here, pltpu.roll(e, k, 1) if k else e, to_left)
+                to_right = jnp.where(here, pltpu.roll(e, k + 1, 1), to_right)
+            pk[0, rb, hw:hw + PAD, :] = to_left
+            pk[1, rb, hw:hw + PAD, :] = to_right
+            for side, has, target in z_sides:
+                @pl.when(has)
+                def _():
+                    pk_copy(side, target, rb).start()
+
+        def pack_ends():
+            for n, lo in ((0, 0), (1, height - PAD)):
+                hk[n] = shifted_rows(lo, PAD)[:, :half]
+            for side, has, target in z_sides:
+                @pl.when(has)
+                def _():
+                    hk_copy(side, target).start()
+
+        def unpack(rb):
+            for side, has, target in z_sides:
+                @pl.when(has)
+                def _():
+                    pk_arrival(side, target, rb).wait_recv()
+            lo = pl.multiple_of(rb * half + PAD, PAD)
+            from_left, from_right = pr[0, rb, 0:hw, :], pr[1, rb, 0:hw, :]
+            for n in range(2):
+                start = lo + n * hw
+                rolled = shifted_rows(start, hw)
+                m = rolled[:, :half]
+                fl = pltpu.roll(from_left, hw, 1) if n else from_left
+                fr = from_right if n else pltpu.roll(from_right, hw, 1)
+                pe[pl.ds(start, hw), half:2 * half] = jnp.where(low_half, fl, m)
+                pe[pl.ds(start, hw), 2 * half:3 * half] = rolled[:, half:]
+                pe[pl.ds(start, hw), 3 * half:4 * half] = jnp.where(low_half, m, fr)
+            cl, cr = pr[0, rb, hw:hw + PAD, :], pr[1, rb, hw:hw + PAD, :]
+            for k in range(half // PAD):
+                pe[pl.ds(lo + k * PAD, PAD), 0:half] = pltpu.roll(cl, half - 1 - k, 1)
+                pe[pl.ds(lo + k * PAD, PAD), 4 * half:5 * half] = pltpu.roll(cr, half - k, 1) if k else cr
+
+        def unpack_ends():
+            for side, has, target in z_sides:
+                @pl.when(has)
+                def _():
+                    hk_arrival(side, target).wait_recv()
+            low8 = lane8 < hw
+            for n, lo in ((0, 0), (1, height - PAD)):
+                rolled = shifted_rows(lo, PAD)
+                m = rolled[:, :half]
+                pe[lo:lo + PAD, half:2 * half] = jnp.where(low8, hr[0, n], m)
+                pe[lo:lo + PAD, 2 * half:3 * half] = rolled[:, half:]
+                pe[lo:lo + PAD, 3 * half:4 * half] = jnp.where(low8, m, hr[1, n])
+
+        wide = (strips + 2) * half
+        step = 2 * PAD
+
+        def weigh(rb):
+            @pl.loop(0, half // step)
+            def _(c):
+                q = pl.multiple_of(c * step, step)
+                lo = pl.multiple_of(rb * half + PAD + q, PAD)
+                block = pe[pl.ds(lo - PAD, step + 2 * PAD), half:wide - half]
+                line = pe[pl.ds(lo, step), :]
+                mid = block[PAD:PAD + step]
+                fx = harmonic(block[PAD - 1:PAD + step], block[PAD:PAD + step + 1])
+                fy = harmonic(line, pltpu.roll(line, wide - 1, 1))
+                east, west = fx[1:], fx[:-1]
+                north = fy[:, half:wide - half]
+                south = pltpu.roll(fy, 1, 1)[:, half:wide - half]
+                diagonal = east + west + north + south
+                scale = relaxation / jnp.where(diagonal > 0, diagonal, 1.0)
+                for n, face in enumerate((east, west, north, south)):
+                    w[n, rb, pl.ds(q, step), :] = face * scale
 
         peers = sum(jnp.where(has, 1, 0) for _, has, _t in z_sides + x_sides)
         pl.semaphore_wait(barrier, peers)
 
+        for side, has, target in x_sides:
+            @pl.when(has)
+            def _():
+                row_copy(side, target).start()
+        own.wait()
+
+        @pl.loop(1, nx)
+        def _(rb):
+            pack(rb)
+
+        for side, has, target in x_sides:
+            @pl.when(has)
+            def _():
+                row_arrival(side, target).wait_recv()
+
+        @pl.loop(0, 2)
+        def _(n):
+            pack(n * nx)
+
+        pack_ends()
+
+        @pl.loop(1, 4)
+        def _(rb):
+            unpack(rb)
+
+        weigh(need_1[0][0])
+
+        def finish(it, k, i, ready):
+            rb = pick(k, ready)
+
+            @pl.when(rb >= 0)
+            def _():
+                partial(it, rb)
+                z_send(it, rb)
+
+            @pl.when(k >= nx - 2)
+            def _():
+                partial(it, jnp.where(i == 0, 0, nx))
+
+            @pl.when(k == nx - 2)
+            def _():
+                x_send(it, 0)
+
+            @pl.when(k == nx - 1)
+            def _():
+                x_send(it, 1)
+
+        next_pe = [4 + k for k in range(nx - 4)] + [0, nx, -1, -1]
+
         @pl.loop(0, nx)
         def _(k):
-            i = row1(k)
+            i = pick(k, rows_1)
             a_copy(i).wait()
-
-            @pl.when(k == 0)
-            def _():
-                w_wait(0)
-                w_wait(1)
-
-            @pl.when(k == 1)
-            def _():
-                w_wait(nx - 1)
-                w_wait(nx)
-
-            @pl.when((k >= 2) & (k < nx - 1))
-            def _():
-                w_wait(i + 1)
-
+            nxt = pick(k, next_pe)
+
+            @pl.when(nxt >= 0)
+            def _():
+                unpack(nxt)
+
+            @pl.when(k == nx - 2)
+            def _():
+                unpack_ends()
+
+            weigh(pick(k, [n[-1] for n in need_1]))
             smooth_row(i, True)
-
-            @pl.when(k == 0)
-            def _():
-                partial(0, 0)
-                x_send(0, 0)
-
-            @pl.when(k == 1)
-            def _():
-                partial(0, last)
-                x_send(0, 1)
-
-            @pl.when(k >= 2)
-            def _():
-                partial(0, i)
-                z_send(0, i)
-
-            @pl.when(k == nx - 1)
-            def _():
-                partial(0, nx - 1)
-                z_send(0, nx - 1)
+            finish(0, k, i, ready_1)
 
         x_add(0, 0)
         z_send(0, 0)
         x_add(0, 1)
         z_send(0, last)
 
-        invert(0, 1)
+        invert(0, need_2[0][0])
 
         @pl.loop(0, nx)
         def _(k):
-            i = jnp.where(k < nx - 2, k + 1, jnp.where(k == nx - 2, 0, nx - 1))
-            invert(0, jnp.where(k < nx - 2, k + 2, jnp.where(k == nx - 2, 0, nx)))
+            i = pick(k, rows_2)
+            invert(0, pick(k, [n[-1] for n in need_2]))
             normalise(i, b, None)
             smooth_row(i, False)
-
-            @pl.when((k >= 1) & (k < nx - 2))
-            def _():
-                partial(1, i)
-                z_send(1, i)
-
-            @pl.when(k >= nx - 2)
-            def _():
-                rb = jnp.where(k == nx - 2, 1, nx - 1)
-                partial(1, rb)
-                z_send(1, rb)
-                partial(1, jnp.where(k == nx - 2, 0, nx))
-
-            @pl.when(k == nx - 2)
-            def _():
-                x_send(1, 0)
-
-            @pl.when(k == nx - 1)
-            def _():
-                x_send(1, 1)
+            finish(1, k, i, ready_2)
 
         x_add(1, 0)
         z_send(1, 0)
         x_add(1, 1)
         z_send(1, last)
 
-        invert(1, 2)
+        invert(1, need_2[0][-1])
 
         @pl.loop(0, nx)
         def _(k):
-            n = nx - 4
-            i = jnp.where(k < n, k + 2, jnp.where(k == n, 1, jnp.where(
-                k == n + 1, nx - 2, jnp.where(k == n + 2, 0, nx - 1))))
-            rb = jnp.where(k < n, k + 3, jnp.where(k == n, 1, jnp.where(
-                k == n + 1, nx - 1, jnp.where(k == n + 2, 0, nx))))
-            invert(1, rb)
+            i = pick(k, rows_2)
+            invert(1, pick(k, [need_2[0][0]] + [n[-1] for n in need_2[1:]]))
             normalise(i, d, a)
             o_copy(i).start()
 
@@ -344,6 +482,13 @@
                 def _(rb):
                     for it in range(ITERS):
                         z_copy(it, side, target, rb).wait_send()
+                    pk_copy(side, target, rb).wait_send()
+                hk_copy(side, target).wait_send()
+
+        for side, has, target in x_sides:
+            @pl.when(has)
+            def _():
+                row_copy(side, target).wait_send()
 
     return kernel
 
@@ -352,8 +497,7 @@
     nx, ny, full, _ = basis.shape
     half = full // 2
     size_x, size_y = lax.axis_size("gx"), lax.axis_size("gy")
-    padded = padded_2(permeability, (("gx", 0), ("gy", 1)), half // 2 + 1)
-    weights = scaled_couplings(padded)
+    height = permeability.shape[0] + half + 2 * PAD
     f32 = jnp.float32
     strips = ny + 1
     scratch = [
@@ -365,24 +509,36 @@
         pltpu.VMEM((nx + 1, half, strips * half), f32),
         pltpu.VMEM((ITERS, 2, nx + 1, half, half), f32),
         pltpu.VMEM((ITERS, 2, strips, half, half), f32),
+        pltpu.VMEM((height, full), f32),
+        pltpu.VMEM((height, (strips + 2) * half), f32),
+        pltpu.VMEM((2, nx + 1, half // 2 + PAD, half), f32),
+        pltpu.VMEM((2, nx + 1, half // 2 + PAD, half), f32),
+        pltpu.VMEM((2, PAD, half), f32),
+        pltpu.VMEM((2, 2, PAD, half), f32),
         pltpu.SemaphoreType.DMA((nx,)),
-        pltpu.SemaphoreType.DMA((4, nx + 1)),
+        pltpu.SemaphoreType.DMA,
         pltpu.SemaphoreType.DMA((nx,)),
         pltpu.SemaphoreType.DMA((ITERS, 2, nx + 1)),
         pltpu.SemaphoreType.DMA((ITERS, 2, nx + 1)),
         pltpu.SemaphoreType.DMA((ITERS, 2)),
         pltpu.SemaphoreType.DMA((ITERS, 2)),
+        pltpu.SemaphoreType.DMA((2, nx + 1)),
+        pltpu.SemaphoreType.DMA((2, nx + 1)),
+        pltpu.SemaphoreType.DMA((2,)),
+        pltpu.SemaphoreType.DMA((2,)),
+        pltpu.SemaphoreType.DMA((2,)),
+        pltpu.SemaphoreType.DMA((2,)),
     ]
     return pl.pallas_call(
         make_kernel(nx, ny, size_x, size_y, half),
         out_shape=jax.ShapeDtypeStruct(basis.shape, f32),
-        in_specs=[pl.BlockSpec(memory_space=pl.ANY)] * 5,
+        in_specs=[pl.BlockSpec(memory_space=pl.ANY)] * 2,
         out_specs=pl.BlockSpec(memory_space=pl.ANY),
         scratch_shapes=scratch,
         compiler_params=pltpu.CompilerParams(
             collective_id=0, has_side_effects=True, vmem_limit_bytes=48 * 1024 * 1024),
         name="smoothing",
-    )(*weights, basis)
+    )(permeability, basis)
 
 
 def solution(mesh):

time: 76.2 us -> 50.5 us (0.66)
  the two profiles are of different devices: /device:TPU:0 before, /device:TPU:4 now
where the time goes in v2:
time: 50.5 us; the launch traced here: 50.1 us
  Pallas kernels  46.9 us (93%)
  local copies, waits for them, and re-layouts  3.24 us (6%)
    pallas_call x1, Pallas kernels, local(): pl.pallas_call(make_kernel(nx, ny, size_x, size_y, half), out_shape=jax.S...  46.9 us
    unnamed x3, local copies, waits for them, and re-layouts  3.24 us

profile of v2, /device:TPU:4, one launch (start us, length us, event | category | flops | bytes accessed | tf_op | source)
XLA Modules:
  0.0 50.1 jit_solution(6903591762766272998)
XLA Ops:
  0.0 0.0 copy-start
  0.0 1.2 %copy-done = f32[1024,256]{1,0:T(8,128)S(1)} copy-done((f32[1024,256]{1,0:T(8,128)S(1)}, f32[1024,256]{1,0:T(8,128)}, u32[]{:S(2)}) %copy-start) | copy-done | bytes 1048600
  1.2 46.9 %smoothing.1 = f32[8,2,256,256]{3,2,1,0:T(8,128)S(1)} custom-call(f32[1024,256]{1,0:T(8,128)S(1)} %copy-done, f32[8,2,256,256]{3,2,1,0:T(8,128)} %refs_1_.1), custom_call_target="tpu_custom_call" | custom-call | tf_op jit(solution)/shard_map/smoothing/pallas_call | solution.py:532
  48.1 2.0 %copy.4 = f32[8,2,256,256]{3,2,1,0:T(8,128)} copy(f32[8,2,256,256]{3,2,1,0:T(8,128)S(1)} %smoothing.1) | data formatting | bytes 8388608
Async XLA Ops:
  0.0 1.2 %copy-start = (f32[1024,256]{1,0:T(8,128)S(1)}, f32[1024,256]{1,0:T(8,128)}, u32[]{:S(2)}) copy-start(f32[1024,256]{1,0:T(8,128)} %refs_0_.1) | copy-start | bytes 3145732

commit v3 on v2

--- a/solution.py
+++ b/solution.py
@@ -10,10 +10,6 @@
 relaxation = 2.0 / 3.0
 PAD = 8
 CH = 32
-
-
-def harmonic(left, right):
-    return 2.0 * left * right / jnp.maximum(left + right, 1e-30)
 
 
 def pick(k, table):
@@ -355,21 +351,23 @@
         step = 2 * PAD
 
         def weigh(rb):
-            @pl.loop(0, half // step)
+            @pl.loop(0, half // step, unroll=4)
             def _(c):
                 q = pl.multiple_of(c * step, step)
                 lo = pl.multiple_of(rb * half + PAD + q, PAD)
                 block = pe[pl.ds(lo - PAD, step + 2 * PAD), half:wide - half]
                 line = pe[pl.ds(lo, step), :]
                 mid = block[PAD:PAD + step]
-                fx = harmonic(block[PAD - 1:PAD + step], block[PAD:PAD + step + 1])
-                fy = harmonic(line, pltpu.roll(line, wide - 1, 1))
-                east, west = fx[1:], fx[:-1]
-                north = fy[:, half:wide - half]
-                south = pltpu.roll(fy, 1, 1)[:, half:wide - half]
-                diagonal = east + west + north + south
-                scale = relaxation / jnp.where(diagonal > 0, diagonal, 1.0)
-                for n, face in enumerate((east, west, north, south)):
+                east = block[PAD + 1:PAD + 1 + step]
+                west = block[PAD - 1:PAD - 1 + step]
+                north = pltpu.roll(line, wide - 1, 1)[:, half:wide - half]
+                south = pltpu.roll(line, 1, 1)[:, half:wide - half]
+                se, sw, sn, ss = mid + east, mid + west, mid + north, mid + south
+                across, along = sn * ss, se * sw
+                ne, nw = east * sw * across, west * se * across
+                nn, ns = north * ss * along, south * sn * along
+                scale = relaxation / jnp.maximum((ne + nw) + (nn + ns), 1e-30)
+                for n, face in enumerate((ne, nw, nn, ns)):
                     w[n, rb, pl.ds(q, step), :] = face * scale
 
         peers = sum(jnp.where(has, 1, 0) for _, has, _t in z_sides + x_sides)
@@ -532,7 +530,7 @@
     return pl.pallas_call(
         make_kernel(nx, ny, size_x, size_y, half),
         out_shape=jax.ShapeDtypeStruct(basis.shape, f32),
-        in_specs=[pl.BlockSpec(memory_space=pl.ANY)] * 2,
+        in_specs=[pl.BlockSpec(memory_space=pltpu.HBM)] * 2,
         out_specs=pl.BlockSpec(memory_space=pl.ANY),
         scratch_shapes=scratch,
         compiler_params=pltpu.CompilerParams(

time: 50.5 us -> 43.1 us (0.85)
  Pallas kernels: 46.9 us -> 39.7 us
    pallas_call x1, Pallas kernels: 46.9 us -> 39.7 us  [local(): pl.pallas_call(make_kernel(nx, ny, size_x, size_y, half), out_shape=jax.S...]
where the time goes in v3:
time: 43.1 us; the launch traced here: 43 us
  Pallas kernels  39.7 us (92%)
  local copies, waits for them, and re-layouts  3.24 us (8%)
    pallas_call x1, Pallas kernels, local(): pl.pallas_call(make_kernel(nx, ny, size_x, size_y, half), out_shape=jax.S...  39.7 us
    unnamed x3, local copies, waits for them, and re-layouts  3.24 us

profile of v3, /device:TPU:4, one launch (start us, length us, event | category | flops | bytes accessed | tf_op | source)
XLA Modules:
  0.0 43.0 jit_solution(1649816686191303319)
XLA Ops:
  0.0 0.0 copy-start
  0.0 1.2 %copy-done = f32[1024,256]{1,0:T(8,128)S(1)} copy-done((f32[1024,256]{1,0:T(8,128)S(1)}, f32[1024,256]{1,0:T(8,128)}, u32[]{:S(2)}) %copy-start) | copy-done | bytes 1048600
  1.2 39.7 %smoothing.1 = f32[8,2,256,256]{3,2,1,0:T(8,128)S(1)} custom-call(f32[1024,256]{1,0:T(8,128)S(1)} %copy-done, f32[8,2,256,256]{3,2,1,0:T(8,128)} %refs_1_.1), custom_call_target="tpu_custom_call" | custom-call | tf_op jit(solution)/shard_map/smoothing/pallas_call | solution.py:530
  40.9 2.0 %copy.4 = f32[8,2,256,256]{3,2,1,0:T(8,128)} copy(f32[8,2,256,256]{3,2,1,0:T(8,128)S(1)} %smoothing.1) | data formatting | bytes 8388608
Async XLA Ops:
  0.0 1.2 %copy-start = (f32[1024,256]{1,0:T(8,128)S(1)}, f32[1024,256]{1,0:T(8,128)}, u32[]{:S(2)}) copy-start(f32[1024,256]{1,0:T(8,128)} %refs_0_.1) | copy-start | bytes 3145732

commit v4 on v3

--- a/solution.py
+++ b/solution.py
@@ -351,7 +351,7 @@
         step = 2 * PAD
 
         def weigh(rb):
-            @pl.loop(0, half // step, unroll=4)
+            @pl.loop(0, half // step, unroll=8)
             def _(c):
                 q = pl.multiple_of(c * step, step)
                 lo = pl.multiple_of(rb * half + PAD + q, PAD)
@@ -536,7 +536,7 @@
         compiler_params=pltpu.CompilerParams(
             collective_id=0, has_side_effects=True, vmem_limit_bytes=48 * 1024 * 1024),
         name="smoothing",
-    )(permeability, basis)
+    )(*[pltpu.with_memory_space_constraint(x, pltpu.HBM) for x in (permeability, basis)])
 
 
 def solution(mesh):

time: 43.1 us -> 41.6 us (0.965); the launches traced: 43 us -> 41 us
  local copies, waits for them, and re-layouts: 3.24 us -> 2.02 us
  Pallas kernels: 39.7 us -> 39 us
    unnamed x3 -> x1, local copies, waits for them, and re-layouts: 3.24 us -> 2.02 us
    pallas_call x1, Pallas kernels: 39.7 us -> 39 us  [local(): pl.pallas_call(make_kernel(nx, ny, size_x, size_y, half), out_shape=jax.S...]
where the time goes in v4:
time: 41.6 us; the launch traced here: 41 us
  Pallas kernels  39 us (94%)
  local copies, waits for them, and re-layouts  2.02 us (5%)
    pallas_call x1, Pallas kernels, local(): pl.pallas_call(make_kernel(nx, ny, size_x, size_y, half), out_shape=jax.S...  39 us
    unnamed x1, local copies, waits for them, and re-layouts  2.02 us

profile of v4, /device:TPU:4, one launch (start us, length us, event | category | flops | bytes accessed | tf_op | source)
XLA Modules:
  0.0 41.0 jit_solution(15383955284022265800)
XLA Ops:
  0.0 39.0 %smoothing.1 = f32[8,2,256,256]{3,2,1,0:T(8,128)S(1)} custom-call(f32[1024,256]{1,0:T(8,128)} %refs_0_.1, f32[8,2,256,256]{3,2,1,0:T(8,128)} %refs_1_.1), custom_call_target="tpu_custom_call" | custom-call | tf_op jit(solution)/shard_map/smoothing/pallas_call | solution.py:530
  39.0 2.0 %copy.4 = f32[8,2,256,256]{3,2,1,0:T(8,128)} copy(f32[8,2,256,256]{3,2,1,0:T(8,128)S(1)} %smoothing.1) | data formatting | bytes 8388608
